TPU v7x, 256 devices: a whole 4x4x8 slice. The times are simulated.
256 devices in a mesh: seq: 32 (over y, z), nb: 8 (over x, core).
Axes of the slice: x: 4, y: 4, z: 8, core: 2. Of those that a mesh axis runs over, the one named last changes fastest.
Arguments:
- q_self: bfloat16 [8192, 4096], P('seq', 'nb'), may hold values from -6 to 6
- k_self: bfloat16 [8192, 4096], P('seq', 'nb'), may hold values from -6 to 6
- v_self: bfloat16 [8192, 4096], P('seq', 'nb'), may hold values from -6 to 6
- q_cca: bfloat16 [8192, 4096], P('seq', 'nb'), may hold values from -6 to 6
- memory: bfloat16 [8192, 2, 1024], P('seq'), may hold values from -6 to 6
- database: bfloat16 [65536, 2048], P(('seq', 'nb')), may hold values from -6 to 6
- nbr_block: int32 [2048], P(('seq', 'nb')), may hold values from 0 to 127, as said below
- span_offset: int32 [128], P('seq'), may hold values from 1 to 63
- enc_query: bfloat16 [2048, 1024], P('seq'), may hold values from -0.1355122 to 0.1355122
- enc_out: bfloat16 [1024, 2048], P('seq'), may hold values from -0.1875 to 0.1875
- enc_gain: float32 [2048], replicated, may hold values from 0.5 to 1.5
- cca_kv: bfloat16 [2048, 2, 4096], P(None, None, 'nb'), may hold values from -0.134535646 to 0.134535646
Outputs:
- attended: bfloat16 [8192, 4096], P('seq', 'nb')
Inputs may be any that keep to these rules, and one draw needn't show every extreme that they name: `nbr_block`: block ids are local to a group of 8 devices along nb; the owner of id g is nb index g // 16. Among the 8 requests of one device at most 3 name blocks of one owner, and exactly 3 name blocks of some owner.
All inputs are finite; a program needn't handle non-finite values.
Results may differ from a plain program's by a relative error of at most 0.0041.
Values may be sent and summed in bfloat16 or wider, within the bound.
No kernel may reach another device: no remote copies, remote signals or barrier semaphores. Data moves between devices by JAX's collectives and lax.ppermute only.
A program may use at most 192 MiB of HBM per device.

v0:
```python
import jax
import jax.numpy as jnp
from jax import lax
from jax.sharding import PartitionSpec as P

HD = 128
E = 2048
SPAN = 64
K = 2
R = 128
BLK = 16
masked_score = -1e30


def laid_out(pieces, dim):
    dims = list(pieces.shape[1:])
    dims[dim] *= pieces.shape[0]
    return jnp.moveaxis(pieces, 0, dim).reshape(dims)


def gather_together(arrays, axis, dims):
    ravelled = jnp.concatenate([a.reshape(-1) for a in arrays])
    lines, at, gathered = (lax.all_gather(ravelled, axis), 0, [])
    for a, dim in zip(arrays, dims):
        pieces = lines[:, at : at + a.size].reshape(-1, *a.shape)
        gathered.append(laid_out(pieces, dim))
        at += a.size
    return tuple(gathered)


def passed_along(block, axis, distance):
    devices = range(lax.axis_size(axis))
    route = [(i - distance, i) for i in devices if i - distance in devices]
    return lax.ppermute(block, axis, route)


def local(
    q_self,
    k_self,
    v_self,
    q_cca,
    memory,
    database,
    nbr_block,
    span_offset,
    enc_query,
    enc_out,
    enc_gain,
    cca_kv,
):
    tokens_here = q_self.shape[0]
    head_cols = q_self.shape[1]
    head_count = head_cols // HD
    score_scale = HD ** (-0.5)
    query_start = lax.axis_index("seq") * tokens_here
    query_pos = query_start + jnp.arange(tokens_here, dtype=jnp.int32)
    queries = q_self.reshape(tokens_here, head_count, HD)
    key_part = lax.all_gather(k_self, "seq", axis=0, tiled=True)
    value_part = lax.all_gather(v_self, "seq", axis=0, tiled=True)
    key_count = key_part.shape[0]
    scores = (
        jnp.einsum(
            "qhd,khd->hqk",
            queries,
            key_part.reshape(key_count, head_count, HD),
            preferred_element_type=jnp.float32,
        )
        * score_scale
    )
    key_pos = jnp.arange(key_count, dtype=jnp.int32)
    allowed = (key_pos[None, :] <= query_pos[:, None])[None]
    scores = jnp.where(allowed, scores, masked_score)
    old_max = jnp.full((head_count, tokens_here), masked_score, jnp.float32)
    new_max = jnp.maximum(old_max, jnp.max(scores, axis=2))
    weights_raw = jnp.where(allowed, jnp.exp(scores - new_max[:, :, None]), 0.0)
    new_sum = jnp.sum(weights_raw, axis=2)
    added = jnp.einsum(
        "hqk,khd->hqd",
        weights_raw.astype(jnp.bfloat16),
        value_part.reshape(key_count, head_count, HD),
        preferred_element_type=jnp.float32,
    )
    self_out = (added / new_sum[:, :, None]).transpose(1, 0, 2).reshape(tokens_here, head_cols)
    query_full, output_full = gather_together((enc_query, enc_out), "seq", (0, 0))
    enc_heads = memory.shape[2] // HD
    memory_keys = memory[:, 0].reshape(tokens_here, enc_heads, HD)
    memory_values = memory[:, 1].reshape(tokens_here, enc_heads, HD)
    key_span = jnp.arange(tokens_here, dtype=jnp.int32) // SPAN
    key_open = jnp.arange(tokens_here, dtype=jnp.int32) % SPAN < jnp.repeat(span_offset, SPAN)
    request_count = nbr_block.shape[0]
    owners = lax.axis_size("nb")
    db_count = database.shape[0] // BLK
    capacity = max(2, 3 * request_count // owners)
    owner_ids = nbr_block // db_count
    local_block = nbr_block % db_count
    owner_hits = (owner_ids[:, None] == jnp.arange(owners, dtype=jnp.int32)[None, :]).astype(
        jnp.int32
    )
    rank_within = jnp.sum((jnp.cumsum(owner_hits, axis=0) - 1) * owner_hits, axis=1)
    slot_index = owner_ids * capacity + rank_within
    blocks_span = K * (R // BLK)
    request_place = (
        lax.axis_index("nb") * request_count + jnp.arange(request_count, dtype=jnp.int32) + 1
    )
    request_span = (request_place - 1) // blocks_span
    slot_match = slot_index[None, :] == jnp.arange(owners * capacity, dtype=jnp.int32)[:, None]
    sent_block = jnp.sum(jnp.where(slot_match, local_block[None, :], 0), axis=1)
    sent_span = jnp.sum(jnp.where(slot_match, request_span[None, :], 0), axis=1)
    sent_place = jnp.sum(jnp.where(slot_match, request_place[None, :], 0), axis=1)
    packed = jnp.stack([sent_block, sent_span, sent_place], axis=-1).reshape(owners, capacity, 3)
    db_blocks = database.reshape(db_count, BLK, E)
    request_rows = lax.all_to_all(packed, "nb", split_axis=0, concat_axis=0, tiled=True)
    slot_count = request_rows.shape[1]
    fetched = db_blocks[request_rows[:, :, 0].reshape(-1)].reshape(-1, E)
    exchanged = lax.all_to_all(
        fetched.reshape(owners, slot_count, BLK, E), "nb", split_axis=0, concat_axis=0, tiled=True
    )
    weight_kv = cca_kv.reshape(E, 2 * head_cols)
    own_rows = exchanged.reshape(owners * capacity, BLK, E)[slot_index].reshape(
        request_count * BLK, E
    )
    row_total = own_rows.shape[0]
    wide = own_rows.astype(jnp.float32)
    normed = wide * lax.rsqrt(jnp.mean(wide * wide, axis=1, keepdims=True) + 1e-06) * enc_gain
    enc_q = (
        jnp.dot(normed.astype(jnp.bfloat16), query_full, preferred_element_type=jnp.float32)
        * score_scale
    ).astype(jnp.bfloat16)
    scores = jnp.einsum(
        "nhd,khd->hnk",
        enc_q.reshape(row_total, enc_heads, HD),
        memory_keys,
        preferred_element_type=jnp.float32,
    )
    allowed = ((key_span[None, :] == jnp.repeat(request_span, BLK)[:, None]) & key_open[None, :])[
        None
    ]
    scores = jnp.where(allowed, scores, masked_score)
    row_max = jnp.max(scores, axis=2, keepdims=True)
    weights_raw = jnp.where(allowed, jnp.exp(scores - row_max), 0.0)
    totals = jnp.sum(weights_raw, axis=2)
    context = jnp.einsum(
        "hnk,khd->nhd",
        weights_raw.astype(jnp.bfloat16),
        memory_values,
        preferred_element_type=jnp.float32,
    )
    context = (
        (context / totals.T[:, :, None]).astype(jnp.bfloat16).reshape(row_total, enc_heads * HD)
    )
    own_rows = (wide + jnp.dot(context, output_full, preferred_element_type=jnp.float32)).astype(
        jnp.bfloat16
    )
    group_kv = jnp.dot(
        lax.all_gather(own_rows, "nb", axis=0, tiled=True),
        weight_kv,
        preferred_element_type=jnp.float32,
    ).astype(jnp.bfloat16)
    span_count = span_offset.shape[0]
    group_kv = group_kv.reshape(span_count, K * R, 2 * head_cols)
    before = passed_along(group_kv[-1], "seq", 1)
    stacked = jnp.concatenate([before[None], group_kv], axis=0)
    cross_queries = q_cca.reshape(span_count, SPAN, head_count, HD)

    def attend_block(kv_set):
        key_rows = kv_set[:, :, :head_cols].reshape(span_count, K * R, head_count, HD)
        value_rows = kv_set[:, :, head_cols:].reshape(span_count, K * R, head_count, HD)
        scores = (
            jnp.einsum(
                "ichd,ikhd->ihck", cross_queries, key_rows, preferred_element_type=jnp.float32
            )
            * score_scale
        )
        row_max = jnp.max(scores, axis=3, keepdims=True)
        weights_raw = jnp.exp(scores - row_max)
        totals = jnp.sum(weights_raw, axis=3)
        summed = jnp.einsum(
            "ihck,ikhd->ichd",
            weights_raw.astype(jnp.bfloat16),
            value_rows,
            preferred_element_type=jnp.float32,
        )
        return summed / totals.transpose(0, 2, 1)[:, :, :, None]

    own_part = attend_block(stacked[1:])
    earlier = attend_block(stacked[:-1])
    see_own = (jnp.arange(SPAN, dtype=jnp.int32)[None, :] >= span_offset[:, None])[:, :, None, None]
    cca_out = jnp.where(see_own, own_part, earlier).reshape(tokens_here, head_cols)
    return (self_out + cca_out).astype(jnp.bfloat16)


def solution(mesh):
    in_specs = (
        P("seq", "nb"),
        P("seq", "nb"),
        P("seq", "nb"),
        P("seq", "nb"),
        P("seq", None, None),
        P(("seq", "nb"), None),
        P(("seq", "nb")),
        P("seq"),
        P("seq", None),
        P("seq", None),
        P(),
        P(None, None, "nb"),
    )
    out_specs = P("seq", "nb")
    return jax.shard_map(local, mesh=mesh, in_specs=in_specs, out_specs=out_specs, check_vma=False)
```

profile of v0, /device:TPU:1, one launch (start us, length us, event | category | flops | bytes accessed | tf_op | source)
XLA Modules:
  0.0 394.9 jit_solution(3428079595198629862)
XLA Ops:
  6.5 1.1 copy.92
  11.4 10.2 %all_to_all.10 = s32[8,3,3]{1,2,0:T(4,128)S(1)} all-to-all(s32[8,3,3]{1,2,0:T(4,128)S(1)} %copy.65), channel_id=1, replica_groups=mesh['seq'=32,'nb'=8] {'nb'}, dimensions={0} | all-to-all | bytes 576 | tf_op jit(solution)/shard_map/all_to_all | solution.py:112
  21.8 1.8 gather_fusion
  23.6 4.9 %all-to-all-start.1 = ((bf16[8,3,16,2048]{3,2,1,0:T(8,128)(2,1)}), bf16[8,3,16,2048]{3,2,1,0:T(8,128)(2,1)}, u32[]{:S(2)}, u32[]{:S(2)}) async-start(bf16[8,3,16,2048]{3,2,1,0:T(8,128)(2,1)} %bitcast.7), calls=%async_computation.1 | async-start | bytes 3145728 | tf_op jit(solution)/shard_map/all_to_all | solution.py:115
  28.5 1.8 copy.61
  30.4 1.5 fusion.58
  31.9 2.0 copy.69
  35.2 14.0 %all-to-all-done.1 = bf16[8,3,16,2048]{3,2,1,0:T(8,128)(2,1)} async-done(((bf16[8,3,16,2048]{3,2,1,0:T(8,128)(2,1)}), bf16[8,3,16,2048]{3,2,1,0:T(8,128)(2,1)}, u32[]{:S(2)}, u32[]{:S(2)}) %all-to-all-start.1) | async-done | bytes 1572896 | tf_op jit(solution)/shard_map/all_to_all | solution.py:115
  49.2 2.0 gather_fusion.1
  51.6 59.4 %all-gather.12.cloned.1.call-done = bf16[4194304]{0:T(1024)(128)(2,1)} async-done(((bf16[131072]{0:T(1024)(128)(2,1)}), bf16[4194304]{0:T(1024)(128)(2,1)}) %all-gather.12.cloned.1.call-update) | async-done | bytes 8388624 | tf_op jit(solution)/shard_map/all_gather | solution.py:23
  111.0 8.7 %reshape.343 = bf16[32,131072]{1,0:T(8,128)(2,1)} reshape(bf16[4194304]{0:T(1024)(128)(2,1)} %all-gather.12.cloned.1.call-done) | data formatting | bytes 16777216 | tf_op jit(solution)/shard_map/all_gather | solution.py:23
  119.7 5.8 %fusion.57 = (bf16[32,65536]{1,0:T(8,128)(2,1)}, bf16[32,65536]{1,0:T(8,128)(2,1)}) fusion(bf16[32,131072]{1,0:T(8,128)(2,1)} %reshape.343), kind=kLoop, calls=%fused_computation.103 | loop fusion | bytes 16777216 | tf_op jit(solution)/shard_map/slice | solution.py:25
  125.5 5.6 %reshape_reshape.10 = bf16[2048,1024]{1,0:T(8,128)(2,1)} reshape(bf16[32,65536]{1,0:T(8,128)(2,1)} %get-tuple-element.11) | data formatting | bytes 8388608 | tf_op jit(solution)/shard_map/reshape;reshape | solution.py:18
  131.2 5.7 %reshape_reshape.11 = bf16[1024,2048]{1,0:T(8,128)(2,1)} reshape(bf16[32,65536]{1,0:T(8,128)(2,1)} %get-tuple-element.10) | data formatting | bytes 8388608 | tf_op jit(solution)/shard_map/reshape;reshape | solution.py:18
  136.9 2.9 fusion.22
  141.1 3.8 fusion.7
  144.9 5.4 %copy.93 = bf16[256,8,2,512]{3,1,2,0:T(8,128)(2,1)} copy(bf16[256,8,2,512]{3,2,1,0:T(2,128)(2,1)} %bitcast.99) | data formatting | bytes 8388608
  150.4 1.3 iota_compare_fusion
  151.7 56.8 %all-gather.8.cloned.1.call-done = bf16[8192,512]{1,0:T(8,128)(2,1)} async-done(((bf16[256,512]{1,0:T(8,128)(2,1)}), bf16[8192,512]{1,0:T(8,128)(2,1)}) %all-gather.8.cloned.1.call-update) | async-done | bytes 8388624 | tf_op jit(solution)/shard_map/all_gather | solution.py:59
  208.5 11.3 %copy.64 = bf16[8192,512]{0,1:T(8,128)(2,1)} copy(bf16[8192,512]{1,0:T(8,128)(2,1)} %all-gather.8.cloned.1.call-done) | data formatting | bytes 16777216 | tf_op jit(solution)/shard_map/all_gather | solution.py:59
  219.9 88.1 %all-gather.6.cloned.1.call-done = bf16[8192,512]{0,1:T(8,128)(2,1)} async-done(((bf16[256,512]{0,1:T(8,128)(2,1)}), bf16[8192,512]{0,1:T(8,128)(2,1)}) %all-gather.6.cloned.1.call-update) | async-done | bytes 8388624 | tf_op jit(solution)/shard_map/all_gather | solution.py:58
  307.9 18.8 %fusion.1 = (f32[4,256]{1,0:T(4,128)S(1)}, f32[4,256,8192]{2,1,0:T(8,128)}) fusion(pred[256,8192]{1,0:T(8,128)(4,1)S(1)} %iota_compare_fusion, bf16[8192,4,128]{0,2,1:T(8,128)(2,1)} %bitcast.119, bf16[256,512]{1,0:T(8,128)(2,1)S(1)} %copy-done.9), kind=kOutput, calls=%fused_computation.5 | convolution fusion | flops 2172648448 | bytes 44306432 | tf_op jit(solution)/shard_map/qhd,khd->hqk/dot_general | solution.py:62
  326.8 15.9 %fusion.2 = f32[4,256]{1,0:T(4,128)S(1)} fusion(f32[4,256,8192]{2,1,0:T(8,128)} %get-tuple-element.21, f32[4,256]{1,0:T(4,128)S(1)} %broadcast_maximum_fusion, pred[256,8192]{1,0:T(8,128)(4,1)S(1)} %iota_compare_fusion), kind=kLoop, calls=%fused_computation.6 | loop fusion | flops 41942016 | bytes 35659776 | tf_op jit(solution)/shard_map/reduce_sum | solution.py:76
  342.7 4.0 %all-gather.10.cloned.1.call-done = bf16[1024,2048]{1,0:T(8,128)(2,1)} async-done(((bf16[128,2048]{1,0:T(8,128)(2,1)}), bf16[1024,2048]{1,0:T(8,128)(2,1)}) %all-gather.10.cloned.1.call-update) | async-done | bytes 4194320 | tf_op jit(solution)/shard_map/all_gather | solution.py:155
  346.7 7.9 %convolution_convert_fusion = bf16[1024,1024]{1,0:T(8,128)(2,1)S(1)} fusion(bf16[1024,2048]{1,0:T(8,128)(2,1)} %all-gather.10.cloned.1.call-done, bf16[2048,1024]{1,0:T(8,128)(2,1)} %bitcast.100), kind=kOutput, calls=%fused_computation.13 | convolution fusion | flops 4296015872 | bytes 10485760 | tf_op jit(solution)/shard_map/dot_general | solution.py:154
  354.6 1.3 copy-done.3
  356.0 3.2 collective-permute-start
  359.2 17.6 %fusion.23 = f32[256,4,128]{0,2,1:T(8,128)} fusion(bf16[8192,4,128]{0,2,1:T(8,128)(2,1)} %bitcast.95, f32[4,256,8192]{2,1,0:T(8,128)} %get-tuple-element.21, f32[4,256]{1,0:T(4,128)S(1)} %broadcast_maximum_fusion, pred[256,8192]{1,0:T(8,128)(4,1)S(1)} %iota_compare_fusion, f32[256,4]{0,1:T(4,128)S(1)} %bitcast.118), kind=kOutput, calls=%fused_computation.34 | convolution fusion | flops 2189557760 | bytes 44572672 | tf_op jit(solution)/shard_map/hqk,khd->hqd/dot_general | solution.py:77
  376.8 2.0 copy.81
  378.9 2.8 copy.70
  381.7 1.0 copy.75
  382.7 1.6 pad_maximum_fusion
  (74 shorter events, 11.1 us)
Async XLA Ops:
  6.5 15.2 %copy-start = (bf16[256,2048]{1,0:T(8,128)(2,1)S(1)}, bf16[256,2048]{1,0:T(8,128)(2,1)}, u32[]{:S(2)}) copy-start(bf16[256,2048]{1,0:T(8,128)(2,1)} %param.17) | copy-start | bytes 3145732
  6.5 23.8 %copy-start.2 = (bf16[256,2,1024]{2,1,0:T(2,128)(2,1)S(1)}, bf16[256,2,1024]{2,1,0:T(2,128)(2,1)}, u32[]{:S(2)}) copy-start(bf16[256,2,1024]{2,1,0:T(2,128)(2,1)} %param.16) | copy-start | bytes 3145732
  6.5 28.4 %copy-start.8 = (s32[4]{0:T(128)S(1)}, s32[4]{0:T(128)}, u32[]{:S(2)}) copy-start(s32[4]{0:T(128)} %param.19) | copy-start | bytes 52
  6.5 104.4 %all-gather.12.cloned.1.call-start = ((), (), s32[]{:S(2)}) async-start(), calls=%async_computation.5 | async-start | bytes 8650752 | tf_op jit(solution)/shard_map/all_gather | solution.py:23
  9.3 42.1 %copy-start.7 = (f32[2048]{0:T(1024)S(1)}, f32[2048]{0:T(1024)}, u32[]{:S(2)}) copy-start(f32[2048]{0:T(1024)} %param.22) | copy-start | bytes 24580
  9.3 199.2 %all-gather.8.cloned.1.call-start = ((), (), s32[]{:S(2)}) async-start(), calls=%async_computation.3 | async-start | bytes 8650752 | tf_op jit(solution)/shard_map/all_gather | solution.py:59
  23.6 25.6 %all-to-all-start.1 = ((bf16[8,3,16,2048]{3,2,1,0:T(8,128)(2,1)}), bf16[8,3,16,2048]{3,2,1,0:T(8,128)(2,1)}, u32[]{:S(2)}, u32[]{:S(2)}) async-start(bf16[8,3,16,2048]{3,2,1,0:T(8,128)(2,1)} %bitcast.7), calls=%async_computation.1 | async-start | bytes 3145728 | tf_op jit(solution)/shard_map/all_to_all | solution.py:115
  28.5 279.4 %all-gather.6.cloned.1.call-start = ((), (), s32[]{:S(2)}) async-start(), calls=%async_computation.2 | async-start | bytes 8650752 | tf_op jit(solution)/shard_map/all_gather | solution.py:58
  30.3 316.3 %all-gather.10.cloned.1.call-start = ((), (), s32[]{:S(2)}) async-start(), calls=%async_computation.4 | async-start | bytes 4718592 | tf_op jit(solution)/shard_map/all_gather | solution.py:155
  131.2 9.5 %copy-start.5 = (bf16[256,1,1024]{0,2,1:T(8,128)(2,1)S(1)}, bf16[256,1,1024]{0,2,1:T(8,128)(2,1)}, u32[]{:S(2)}) copy-start(bf16[256,1,1024]{0,2,1:T(8,128)(2,1)} %copy.69) | copy-start | bytes 1572868
  140.7 9.6 %copy-start.6 = (bf16[256,512]{1,0:T(8,128)(2,1)S(1)}, bf16[256,512]{1,0:T(8,128)(2,1)}, u32[]{:S(2)}) copy-start(bf16[256,512]{1,0:T(8,128)(2,1)} %param.15) | copy-start | bytes 786436
  151.7 156.2 %copy-start.9 = (bf16[256,512]{1,0:T(8,128)(2,1)S(1)}, bf16[256,512]{1,0:T(8,128)(2,1)}, u32[]{:S(2)}) copy-start(bf16[256,512]{1,0:T(8,128)(2,1)} %param.12) | copy-start | bytes 786436
  354.6 1.3 copy-start.3
  356.0 25.7 %collective-permute-start = (bf16[256,1024]{1,0:T(8,128)(2,1)S(1)}, bf16[256,1024]{1,0:T(8,128)(2,1)S(1)}, u32[]{:S(2)}, u32[]{:S(2)}) collective-permute-start(bf16[256,1024]{1,0:T(8,128)(2,1)S(1)} %slice.53), channel_id=1, source_target_pairs={{0,8},{8,16},{16,24},{24,32},{32,40},{40,48},{48,56},{56,64},{64,7... | collective-permute-start | bytes 1572872 | tf_op jit(solution)/shard_map/ppermute | solution.py:34
  382.7 5.6 %copy-start.1 = (bf16[256,2048]{1,0:T(8,128)(2,1)S(1)}, bf16[256,2048]{1,0:T(8,128)(2,1)}, u32[]{:S(2)}) copy-start(bf16[256,2048]{1,0:T(8,128)(2,1)} %param.17) | copy-start | bytes 3145732
  384.3 3.3 copy-start.4
Sparse Core Ops, SparseCore 0:
  9.9 101.0 all-gather.11
  113.6 94.9 all-gather.7
  211.0 96.8 all-gather.5
  309.7 36.9 all-gather.9
where the time goes:
time: 396 us; the launch traced here: 395 us
  waiting for transfers between devices  223 us (56%)
  local copies, waits for them, and re-layouts  62.9 us (16%)
  matrix products  54.5 us (14%)
  other arithmetic  22.7 us (6%)
  between operations  13.4 us (3%)
  blocking collectives  10.2 us (3%)
  starting transfers between devices  8.19 us (2%)
    all_gather x1, waiting for transfers between devices, local(): key_part = lax.all_gather(k_self, 'seq', axis=0, tiled=True)  88.1 us
    all_gather x1, waiting for transfers between devices, gather_together(): lines, at, gathered = (lax.all_gather(ravelled, axis), 0, [])  59.4 us
    all_gather x1, waiting for transfers between devices, local(): value_part = lax.all_gather(v_self, 'seq', axis=0, tiled=True)  56.8 us
    dot_general x1, matrix products, local(): jnp.einsum('qhd,khd->hqk', queries, key_part.reshape(key_count, head_coun...  18.8 us
    dot_general x1, matrix products, local(): jnp.einsum('hqk,khd->hqd', weights_raw.astype(jnp.bfloat16), value_part.r...  17.6 us
    reduce_sum x1, other arithmetic, local(): new_sum = jnp.sum(weights_raw, axis=2)  15.9 us
    all_to_all x1, waiting for transfers between devices, local(): lax.all_to_all(fetched.reshape(owners, slot_count, BLK, E), 'nb', split_a...  14 us
    unnamed x25, local copies, waits for them, and re-layouts  11.4 us
  transfers between devices with their start and end apart: 6, of which 5 were waited for; matrix products, arithmetic and copies ran while one was open for 31% of the time, Pallas kernels for 0%

commit v1 on v0

--- a/solution.py
+++ b/solution.py
@@ -55,7 +55,9 @@
     query_start = lax.axis_index("seq") * tokens_here
     query_pos = query_start + jnp.arange(tokens_here, dtype=jnp.int32)
     queries = q_self.reshape(tokens_here, head_count, HD)
-    key_part = lax.all_gather(k_self, "seq", axis=0, tiled=True)
+    key_part = jnp.concatenate(
+        lax.all_to_all(jnp.stack([k_self] * lax.axis_size("seq")), "seq", 0, 0), axis=0
+    )
     value_part = lax.all_gather(v_self, "seq", axis=0, tiled=True)
     key_count = key_part.shape[0]
     scores = (

time: 396 us -> 452 us (1.14)
  local copies, waits for them, and re-layouts: 62.9 us -> 91.4 us
  waiting for transfers between devices: 223 us -> 239 us
  starting transfers between devices: 8.19 us -> 18.1 us
    all_gather x1 -> x0, waiting for transfers between devices: 88.1 us -> none  [local(): key_part = lax.all_gather(k_self, 'seq', axis=0, tiled=True)]
    all_gather x1, waiting for transfers between devices: 59.4 us -> 136 us  [gather_together(): lines, at, gathered = (lax.all_gather(ravelled, axis), 0, [])]
    all_to_all x0 -> x1, waiting for transfers between devices: none -> 53.8 us  [local(): lax.all_to_all(jnp.stack([k_self] * lax.axis_size('seq')), 'seq', 0, 0)]
    all_gather x1, waiting for transfers between devices: 56.8 us -> 34.5 us  [local(): value_part = lax.all_gather(v_self, 'seq', axis=0, tiled=True)]
    another operation x0 -> x2, local copies, waits for them, and re-layouts: none -> 17.7 us  [the longest x1 13.6 us: local(): key_part.reshape(key_count, head_count, HD)]
    all_to_all x0 -> x1, starting transfers between devices: none -> 11.5 us  [local(): lax.all_to_all(jnp.stack([k_self] * lax.axis_size('seq')), 'seq', 0, 0)]
    all_to_all x0 -> x1, local copies, waits for them, and re-layouts: none -> 11.4 us  [local(): lax.all_to_all(jnp.stack([k_self] * lax.axis_size('seq')), 'seq', 0, 0)]
  transfers between devices with their start and end apart: 6 -> 6, of which waited for: 5 -> 4; matrix products, arithmetic and copies ran while one was open for 31% -> 33% of each run, Pallas kernels for 0% -> 0%
where the time goes in v1:
time: 452 us; the launch traced here: 450 us
  waiting for transfers between devices  239 us (53%)
  local copies, waits for them, and re-layouts  91.4 us (20%)
  matrix products  55 us (12%)
  other arithmetic  22.5 us (5%)
  starting transfers between devices  18.1 us (4%)
  between operations  13.4 us (3%)
  blocking collectives  10.2 us (2%)
    all_gather x1, waiting for transfers between devices, gather_together(): lines, at, gathered = (lax.all_gather(ravelled, axis), 0, [])  136 us
    all_to_all x1, waiting for transfers between devices, local(): lax.all_to_all(jnp.stack([k_self] * lax.axis_size('seq')), 'seq', 0, 0)  53.8 us
    all_gather x1, waiting for transfers between devices, local(): value_part = lax.all_gather(v_self, 'seq', axis=0, tiled=True)  34.5 us
    dot_general x1, matrix products, local(): jnp.einsum('qhd,khd->hqk', queries, key_part.reshape(key_count, head_coun...  19.3 us
    dot_general x1, matrix products, local(): jnp.einsum('hqk,khd->hqd', weights_raw.astype(jnp.bfloat16), value_part.r...  17.7 us
    reduce_sum x1, other arithmetic, local(): new_sum = jnp.sum(weights_raw, axis=2)  15.7 us
    all_to_all x1, waiting for transfers between devices, local(): lax.all_to_all(fetched.reshape(owners, slot_count, BLK, E), 'nb', split_a...  14.1 us
    another operation x1, local copies, waits for them, and re-layouts, local(): key_part.reshape(key_count, head_count, HD)  13.6 us
  transfers between devices with their start and end apart: 6, of which 4 were waited for; matrix products, arithmetic and copies ran while one was open for 33% of the time, Pallas kernels for 0%

profile of v1, /device:TPU:1, one launch (start us, length us, event | category | flops | bytes accessed | tf_op | source)
XLA Modules:
  0.0 450.1 jit_solution(2893449387342755766)
XLA Ops:
  10.6 10.2 %all_to_all.15 = s32[8,3,3]{1,2,0:T(4,128)S(1)} all-to-all(s32[8,3,3]{1,2,0:T(4,128)S(1)} %copy.67), channel_id=1, replica_groups=mesh['seq'=32,'nb'=8] {'nb'}, dimensions={0} | all-to-all | bytes 576 | tf_op jit(solution)/shard_map/all_to_all | solution.py:114
  21.0 1.9 gather_fusion
  22.9 4.9 %all-to-all-start.2 = ((bf16[8,3,16,2048]{3,2,1,0:T(8,128)(2,1)}), bf16[8,3,16,2048]{3,2,1,0:T(8,128)(2,1)}, u32[]{:S(2)}, u32[]{:S(2)}) async-start(bf16[8,3,16,2048]{3,2,1,0:T(8,128)(2,1)} %bitcast.6), calls=%async_computation.2 | async-start | bytes 3145728 | tf_op jit(solution)/shard_map/all_to_all | solution.py:117
  29.7 1.5 fusion.58
  31.2 2.0 copy.71
  34.5 14.1 %all-to-all-done.2 = bf16[8,3,16,2048]{3,2,1,0:T(8,128)(2,1)} async-done(((bf16[8,3,16,2048]{3,2,1,0:T(8,128)(2,1)}), bf16[8,3,16,2048]{3,2,1,0:T(8,128)(2,1)}, u32[]{:S(2)}, u32[]{:S(2)}) %all-to-all-start.2) | async-done | bytes 1572896 | tf_op jit(solution)/shard_map/all_to_all | solution.py:117
  48.5 4.2 stack.10
  52.7 11.5 %all-to-all-start = ((bf16[32,256,512]{1,2,0:T(8,128)(2,1)}), bf16[32,256,512]{1,2,0:T(8,128)(2,1)}, u32[]{:S(2)}, u32[]{:S(2)}) async-start(bf16[32,256,512]{1,2,0:T(8,128)(2,1)} %stack.10), calls=%async_computation | async-start | bytes 16777216 | tf_op jit(solution)/shard_map/all_to_all | solution.py:59
  64.2 2.2 gather_fusion.1
  66.8 136.2 %all-gather.9.cloned.1.call-done = bf16[4194304]{0:T(1024)(128)(2,1)} async-done(((bf16[131072]{0:T(1024)(128)(2,1)}), bf16[4194304]{0:T(1024)(128)(2,1)}) %all-gather.9.cloned.1.call-update) | async-done | bytes 8388624 | tf_op jit(solution)/shard_map/all_gather | solution.py:23
  203.1 8.7 %reshape.341 = bf16[32,131072]{1,0:T(8,128)(2,1)} reshape(bf16[4194304]{0:T(1024)(128)(2,1)} %all-gather.9.cloned.1.call-done) | data formatting | bytes 16777216 | tf_op jit(solution)/shard_map/all_gather | solution.py:23
  211.7 5.7 %fusion.57 = (bf16[32,65536]{1,0:T(8,128)(2,1)}, bf16[32,65536]{1,0:T(8,128)(2,1)}) fusion(bf16[32,131072]{1,0:T(8,128)(2,1)} %reshape.341), kind=kLoop, calls=%fused_computation.103 | loop fusion | bytes 16777216 | tf_op jit(solution)/shard_map/slice | solution.py:25
  217.4 5.7 %reshape_reshape.14 = bf16[2048,1024]{1,0:T(8,128)(2,1)} reshape(bf16[32,65536]{1,0:T(8,128)(2,1)} %get-tuple-element.11) | data formatting | bytes 8388608 | tf_op jit(solution)/shard_map/reshape;reshape | solution.py:18
  223.1 5.7 %reshape_reshape.15 = bf16[1024,2048]{1,0:T(8,128)(2,1)} reshape(bf16[32,65536]{1,0:T(8,128)(2,1)} %get-tuple-element.10) | data formatting | bytes 8388608 | tf_op jit(solution)/shard_map/reshape;reshape | solution.py:18
  228.8 2.9 fusion.22
  233.0 3.9 fusion.7
  236.9 5.3 %copy.95 = bf16[256,8,2,512]{3,1,2,0:T(8,128)(2,1)} copy(bf16[256,8,2,512]{3,2,1,0:T(2,128)(2,1)} %bitcast.100) | data formatting | bytes 8388608
  242.4 1.3 iota_compare_fusion
  243.7 53.8 %all-to-all-done = bf16[32,256,512]{1,2,0:T(8,128)(2,1)} async-done(((bf16[32,256,512]{1,2,0:T(8,128)(2,1)}), bf16[32,256,512]{1,2,0:T(8,128)(2,1)}, u32[]{:S(2)}, u32[]{:S(2)}) %all-to-all-start) | async-done | bytes 8388640 | tf_op jit(solution)/shard_map/all_to_all | solution.py:59
  297.6 11.4 %copy.63 = bf16[32,256,512]{1,0,2:T(8,128)(2,1)} copy(bf16[32,256,512]{1,2,0:T(8,128)(2,1)} %all-to-all-done) | data formatting | bytes 16777216 | tf_op jit(solution)/shard_map/all_to_all | solution.py:59
  308.9 13.6 %reshape_reshape.12 = bf16[8192,4,128]{0,2,1:T(8,128)(2,1)} reshape(bf16[32,256,512]{1,0,2:T(8,128)(2,1)} %copy.63) | data formatting | bytes 16777216 | tf_op jit(solution)/shard_map/reshape;reshape | solution.py:67
  322.5 34.5 %all-gather.5.cloned.1.call-done = bf16[8192,512]{1,0:T(8,128)(2,1)} async-done(((bf16[256,512]{1,0:T(8,128)(2,1)}), bf16[8192,512]{1,0:T(8,128)(2,1)}) %all-gather.5.cloned.1.call-update) | async-done | bytes 8388624 | tf_op jit(solution)/shard_map/all_gather | solution.py:61
  357.0 11.3 %copy.66 = bf16[8192,512]{0,1:T(8,128)(2,1)} copy(bf16[8192,512]{1,0:T(8,128)(2,1)} %all-gather.5.cloned.1.call-done) | data formatting | bytes 16777216 | tf_op jit(solution)/shard_map/all_gather | solution.py:61
  368.3 19.3 %fusion.1 = (f32[4,256]{1,0:T(4,128)S(1)}, f32[4,256,8192]{2,1,0:T(8,128)}) fusion(pred[256,8192]{1,0:T(8,128)(4,1)S(1)} %iota_compare_fusion, bf16[8192,4,128]{0,2,1:T(8,128)(2,1)} %reshape_reshape.12, bf16[256,512]{1,0:T(8,128)(2,1)S(1)} %copy-done.9), kind=kOutput, calls=%fused_computation.5 | convolution fusion | flops 2172648448 | bytes 44306432 | tf_op jit(solution)/shard_map/qhd,khd->hqk/dot_general | solution.py:64
  387.6 15.7 %fusion.2 = f32[4,256]{1,0:T(4,128)S(1)} fusion(f32[4,256,8192]{2,1,0:T(8,128)} %get-tuple-element.21, f32[4,256]{1,0:T(4,128)S(1)} %broadcast_maximum_fusion, pred[256,8192]{1,0:T(8,128)(4,1)S(1)} %iota_compare_fusion), kind=kLoop, calls=%fused_computation.6 | loop fusion | flops 41942016 | bytes 35659776 | tf_op jit(solution)/shard_map/reduce_sum | solution.py:78
  403.3 8.0 %convolution_convert_fusion = bf16[1024,1024]{1,0:T(8,128)(2,1)S(1)} fusion(bf16[1024,2048]{1,0:T(8,128)(2,1)} %all-gather.7.cloned.1.call-done, bf16[2048,1024]{1,0:T(8,128)(2,1)} %bitcast.101), kind=kOutput, calls=%fused_computation.13 | convolution fusion | flops 4296015872 | bytes 10485760 | tf_op jit(solution)/shard_map/dot_general | solution.py:156
  411.3 1.3 copy-done.3
  412.6 1.7 collective-permute-start
  414.4 17.7 %fusion.23 = f32[256,4,128]{0,2,1:T(8,128)} fusion(bf16[8192,4,128]{0,2,1:T(8,128)(2,1)} %bitcast.96, f32[4,256,8192]{2,1,0:T(8,128)} %get-tuple-element.21, f32[4,256]{1,0:T(4,128)S(1)} %broadcast_maximum_fusion, pred[256,8192]{1,0:T(8,128)(4,1)S(1)} %iota_compare_fusion, f32[256,4]{0,1:T(4,128)S(1)} %bitcast.119), kind=kOutput, calls=%fused_computation.34 | convolution fusion | flops 2189557760 | bytes 44572672 | tf_op jit(solution)/shard_map/hqk,khd->hqd/dot_general | solution.py:79
  432.1 2.0 copy.83
  434.1 2.8 copy.72
  438.0 1.6 pad_maximum_fusion
  (76 shorter events, 14.2 us)
Async XLA Ops:
  6.5 14.4 %copy-start = (bf16[256,2048]{1,0:T(8,128)(2,1)S(1)}, bf16[256,2048]{1,0:T(8,128)(2,1)}, u32[]{:S(2)}) copy-start(bf16[256,2048]{1,0:T(8,128)(2,1)} %param.17) | copy-start | bytes 3145732
  6.5 23.1 %copy-start.2 = (bf16[256,2,1024]{2,1,0:T(2,128)(2,1)S(1)}, bf16[256,2,1024]{2,1,0:T(2,128)(2,1)}, u32[]{:S(2)}) copy-start(bf16[256,2,1024]{2,1,0:T(2,128)(2,1)} %param.16) | copy-start | bytes 3145732
  6.5 27.7 %copy-start.8 = (s32[4]{0:T(128)S(1)}, s32[4]{0:T(128)}, u32[]{:S(2)}) copy-start(s32[4]{0:T(128)} %param.19) | copy-start | bytes 52
  6.5 196.5 %all-gather.9.cloned.1.call-start = ((), (), s32[]{:S(2)}) async-start(), calls=%async_computation.5 | async-start | bytes 8650752 | tf_op jit(solution)/shard_map/all_gather | solution.py:23
  22.9 25.6 %all-to-all-start.2 = ((bf16[8,3,16,2048]{3,2,1,0:T(8,128)(2,1)}), bf16[8,3,16,2048]{3,2,1,0:T(8,128)(2,1)}, u32[]{:S(2)}, u32[]{:S(2)}) async-start(bf16[8,3,16,2048]{3,2,1,0:T(8,128)(2,1)} %bitcast.6), calls=%async_computation.2 | async-start | bytes 3145728 | tf_op jit(solution)/shard_map/all_to_all | solution.py:117
  27.8 329.2 %all-gather.5.cloned.1.call-start = ((), (), s32[]{:S(2)}) async-start(), calls=%async_computation.3 | async-start | bytes 8650752 | tf_op jit(solution)/shard_map/all_gather | solution.py:61
  52.7 13.9 %copy-start.7 = (f32[2048]{0:T(1024)S(1)}, f32[2048]{0:T(1024)}, u32[]{:S(2)}) copy-start(f32[2048]{0:T(1024)} %param.22) | copy-start | bytes 24580
  52.7 244.8 %all-to-all-start = ((bf16[32,256,512]{1,2,0:T(8,128)(2,1)}), bf16[32,256,512]{1,2,0:T(8,128)(2,1)}, u32[]{:S(2)}, u32[]{:S(2)}) async-start(bf16[32,256,512]{1,2,0:T(8,128)(2,1)} %stack.10), calls=%async_computation | async-start | bytes 16777216 | tf_op jit(solution)/shard_map/all_to_all | solution.py:59
  64.2 339.1 %all-gather.7.cloned.1.call-start = ((), (), s32[]{:S(2)}) async-start(), calls=%async_computation.4 | async-start | bytes 4718592 | tf_op jit(solution)/shard_map/all_gather | solution.py:157
  223.1 9.5 %copy-start.5 = (bf16[256,1,1024]{0,2,1:T(8,128)(2,1)S(1)}, bf16[256,1,1024]{0,2,1:T(8,128)(2,1)}, u32[]{:S(2)}) copy-start(bf16[256,1,1024]{0,2,1:T(8,128)(2,1)} %copy.71) | copy-start | bytes 1572868
  232.6 9.7 %copy-start.6 = (bf16[256,512]{1,0:T(8,128)(2,1)S(1)}, bf16[256,512]{1,0:T(8,128)(2,1)}, u32[]{:S(2)}) copy-start(bf16[256,512]{1,0:T(8,128)(2,1)} %param.15) | copy-start | bytes 786436
  322.5 45.8 %copy-start.9 = (bf16[256,512]{1,0:T(8,128)(2,1)S(1)}, bf16[256,512]{1,0:T(8,128)(2,1)}, u32[]{:S(2)}) copy-start(bf16[256,512]{1,0:T(8,128)(2,1)} %param.12) | copy-start | bytes 786436
  411.3 1.4 copy-start.3
  412.6 24.3 %collective-permute-start = (bf16[256,1024]{1,0:T(8,128)(2,1)S(1)}, bf16[256,1024]{1,0:T(8,128)(2,1)S(1)}, u32[]{:S(2)}, u32[]{:S(2)}) collective-permute-start(bf16[256,1024]{1,0:T(8,128)(2,1)S(1)} %slice.53), channel_id=1, source_target_pairs={{0,8},{8,16},{16,24},{24,32},{32,40},{40,48},{48,56},{56,64},{64,7... | collective-permute-start | bytes 1572872 | tf_op jit(solution)/shard_map/ppermute | solution.py:34
  438.0 5.6 %copy-start.1 = (bf16[256,2048]{1,0:T(8,128)(2,1)S(1)}, bf16[256,2048]{1,0:T(8,128)(2,1)}, u32[]{:S(2)}) copy-start(bf16[256,2048]{1,0:T(8,128)(2,1)} %param.17) | copy-start | bytes 3145732
  439.6 3.3 copy-start.4
Sparse Core Ops, SparseCore 0:
  9.9 193.0 all-gather.8
  205.7 151.2 all-gather.4
  358.9 32.7 all-gather.6
